TPU v7x, 512 devices: a whole 4x8x8 slice. The times are simulated.
512 devices in a mesh: section: 16 (over x_hi, y), fsdp: 32 (over x_lo, z, core).
Axes of the slice: x: 4 (x_hi: 2, x_lo: 2; x = x_hi * 2 + x_lo), y: 8, z: 8, core: 2. Of those that a mesh axis runs over, the one named last changes fastest.
Arguments:
- inputs: bfloat16 [16, 8, 1024, 4096], P('section', None, 'fsdp'), may hold values from -6 to 6
- upstream: bfloat16 [8, 1024, 4096], P(None, 'fsdp'), may hold values from -6 to 6
- weights: bfloat16 [16, 4096, 512], P('section', 'fsdp')
- gain: bfloat16 [16, 4096], P('section', 'fsdp'), may hold values from 0.5 to 1.5
Outputs:
- weight_grad: float32 [16, 4096, 512], P('section', 'fsdp')
- gain_grad: float32 [16, 4096], P('section')
All inputs are finite; a program needn't handle non-finite values.
Results may differ from a plain program's by a relative error of at most 0.035.
Values may be sent and summed in bfloat16 or wider, within the bound.
No kernel may reach another device: no remote copies, remote signals or barrier semaphores. Data moves between devices by JAX's collectives and lax.ppermute only.
A program may use at most 128 MiB of HBM per device.

v0:
```python
import jax
import jax.numpy as jnp
from jax import lax
from jax.sharding import PartitionSpec as P


def passed_along(value, axis, steps):
    count = lax.axis_size(axis)
    leading, last = (max(0, -steps), min(count, count - steps))
    return lax.ppermute(value, axis, [(source, source + steps) for source in range(leading, last)])


def rope_tables(length, head):
    half_head = head // 2
    position = lax.iota(jnp.float32, length)
    freq = jnp.power(500000.0, -2.0 * lax.iota(jnp.float32, half_head) / head)
    angle = position[:, None] * freq[None, :]
    return (jnp.cos(angle), jnp.sin(angle))


def rotate(value_rows, cosine, sine_table):
    half_head = value_rows.shape[-1] // 2
    first = value_rows[..., :half_head]
    second = value_rows[..., half_head:]
    return jnp.concatenate(
        [first * cosine - second * sine_table, second * cosine + first * sine_table], axis=-1
    )


def unrotate(value_rows, cosine, sine_table):
    half_head = value_rows.shape[-1] // 2
    first = value_rows[..., :half_head]
    second = value_rows[..., half_head:]
    return jnp.concatenate(
        [first * cosine + second * sine_table, second * cosine - first * sine_table], axis=-1
    )


def contract_rows(left, right):
    return lax.dot_general(
        left, right, (((0,), (0,)), ((), ())), preferred_element_type=jnp.float32
    )


def contract_cols(left, right):
    return lax.dot_general(
        left, right, (((1,), (1,)), ((), ())), preferred_element_type=jnp.float32
    )


def on_device(inputs, upstream, weights, gain):
    sections = lax.axis_size("section")
    here = lax.axis_index("section")
    micro_count = inputs.shape[1]
    length = inputs.shape[2]
    width = inputs.shape[3]
    head = weights.shape[2] // 4
    rows_here = weights.shape[1]
    groups = lax.axis_size("fsdp")
    gain_rows = jnp.zeros((16, weights.shape[2]), jnp.bfloat16)
    gain_rows = lax.dynamic_update_slice(gain_rows, gain[0][None, :], (0, 0))
    packed = jnp.concatenate([weights[0], gain_rows], axis=0)
    gathered = lax.all_gather(packed, "fsdp", axis=0, tiled=True).reshape(
        groups, rows_here + 16, weights.shape[2]
    )
    w_full = gathered[:, :rows_here, :].reshape(groups * rows_here, weights.shape[2])
    gain_full = gathered[:, rows_here, :rows_here].reshape(groups * rows_here)
    wide_gain = gain_full.astype(jnp.float32)
    w_proj = w_full[:, : 3 * head]
    w_back = w_full[:, 3 * head :]
    xfloat = inputs[0].astype(jnp.float32)
    inv_rms = lax.rsqrt(jnp.mean(xfloat * xfloat, axis=-1, keepdims=True) + 1e-05)
    normed = xfloat * inv_rms
    hidden = (normed * wide_gain).astype(jnp.bfloat16)
    proj = jnp.dot(
        hidden.reshape(micro_count * length, width), w_proj, preferred_element_type=jnp.float32
    ).reshape(micro_count, length, 3 * head)
    cosine, sine_table = rope_tables(length, head)
    query_rows = rotate(proj[..., :head], cosine, sine_table).astype(jnp.bfloat16)
    key_rows = rotate(proj[..., head : 2 * head], cosine, sine_table).astype(jnp.bfloat16)
    value_rows = proj[..., 2 * head :].astype(jnp.bfloat16)
    score_scale = head ** (-0.5)
    causal = lax.broadcasted_iota(jnp.int32, (length, length), 0) >= lax.broadcasted_iota(
        jnp.int32, (length, length), 1
    )
    scores = (
        jnp.einsum("mqh,mkh->mqk", query_rows, key_rows, preferred_element_type=jnp.float32)
        * score_scale
    )
    probs = jax.nn.softmax(jnp.where(causal[None], scores, -1e30), axis=-1)
    probs_b = probs.astype(jnp.bfloat16)
    attended = jnp.einsum(
        "mqk,mkh->mqh", probs_b, value_rows, preferred_element_type=jnp.float32
    ).astype(jnp.bfloat16)

    def tick(tick_no, received, state):
        grad_store, proj_store, gain_acc = state
        micro = tick_no - (sections - 1 - here)
        active = jnp.logical_and(micro >= 0, micro < micro_count)
        clipped = jnp.clip(micro, 0, micro_count - 1)
        slot = jnp.clip(micro, -1, micro_count) + 1
        top_grad = lax.dynamic_index_in_dim(upstream, clipped, 0, keepdims=False)
        grad_in = jnp.where(here == sections - 1, top_grad, received)
        query_m = lax.dynamic_index_in_dim(query_rows, clipped, 0, keepdims=False)
        keys_m = lax.dynamic_index_in_dim(key_rows, clipped, 0, keepdims=False)
        values_m = lax.dynamic_index_in_dim(value_rows, clipped, 0, keepdims=False)
        probs_m = lax.dynamic_index_in_dim(probs, clipped, 0, keepdims=False)
        probs_bm = lax.dynamic_index_in_dim(probs_b, clipped, 0, keepdims=False)
        normed_m = lax.dynamic_index_in_dim(normed, clipped, 0, keepdims=False)
        inv_m = lax.dynamic_index_in_dim(inv_rms, clipped, 0, keepdims=False)
        attention_gradient = jnp.dot(grad_in, w_back, preferred_element_type=jnp.float32).astype(
            jnp.bfloat16
        )
        probability_gradient = contract_cols(attention_gradient, values_m)
        score_gradient = (
            probs_m
            * (
                probability_gradient
                - jnp.sum(probability_gradient * probs_m, axis=-1, keepdims=True)
            )
            * score_scale
        ).astype(jnp.bfloat16)
        query_gradient = jnp.dot(score_gradient, keys_m, preferred_element_type=jnp.float32)
        key_gradient = contract_rows(score_gradient, query_m)
        value_gradient = contract_rows(probs_bm, attention_gradient)
        grad_proj = jnp.concatenate(
            [
                unrotate(query_gradient, cosine, sine_table),
                unrotate(key_gradient, cosine, sine_table),
                value_gradient,
            ],
            axis=-1,
        ).astype(jnp.bfloat16)
        grad_hidden = contract_cols(grad_proj, w_proj)
        gain_term = jnp.sum(grad_hidden * normed_m, axis=0)
        grad_normed = grad_hidden * wide_gain
        grad_x = inv_m * (
            grad_normed - normed_m * jnp.mean(grad_normed * normed_m, axis=-1, keepdims=True)
        )
        grad_out = (grad_in.astype(jnp.float32) + grad_x).astype(jnp.bfloat16)
        grad_store = lax.dynamic_update_index_in_dim(grad_store, grad_in, slot, 0)
        proj_store = lax.dynamic_update_index_in_dim(proj_store, grad_proj, slot, 0)
        gain_acc = gain_acc + jnp.where(active, gain_term, 0.0)
        return (grad_out, (grad_store, proj_store, gain_acc))

    def step_loop(tick_no, carry):
        received, state = carry
        sent, state = tick(tick_no, received, state)
        received = passed_along(sent, "section", -1)
        return (received, state)

    state_start = (
        jnp.zeros((micro_count + 2, length, width), jnp.bfloat16),
        jnp.zeros((micro_count + 2, length, 3 * head), jnp.bfloat16),
        jnp.zeros((width,), jnp.float32),
    )
    total_ticks = sections + micro_count - 1
    received, state = lax.fori_loop(
        0, total_ticks - 1, step_loop, (jnp.zeros((length, width), jnp.bfloat16), state_start)
    )
    leftover, state = tick(total_ticks - 1, received, state)
    grad_store, proj_store, gain_acc = state
    tokens_all = micro_count * length
    grad_flat = grad_store[1 : micro_count + 1].reshape(tokens_all, width)
    proj_flat = proj_store[1 : micro_count + 1].reshape(tokens_all, 3 * head)
    att_flat = attended.reshape(tokens_all, head)
    shard = lax.psum_scatter(
        jnp.concatenate(
            [
                contract_rows(hidden.reshape(tokens_all, width), proj_flat),
                contract_rows(grad_flat, att_flat),
            ],
            axis=1,
        ).astype(jnp.bfloat16),
        "fsdp",
        scatter_dimension=0,
        tiled=True,
    ).astype(jnp.float32)
    gain_sum = jnp.sum(lax.all_gather(gain_acc, "fsdp", axis=0), axis=0)
    return (shard[None], gain_sum[None])


def solution(mesh):
    return jax.shard_map(
        on_device,
        mesh=mesh,
        in_specs=(
            P("section", None, "fsdp", None),
            P(None, "fsdp", None),
            P("section", "fsdp", None),
            P("section", "fsdp"),
        ),
        out_specs=(P("section", "fsdp", None), P("section", None)),
        check_vma=False,
    )
```

profile of v0, /device:TPU:4, one launch (start us, length us, event | category | flops | bytes accessed | tf_op | source)
XLA Modules:
  0.0 805.6 jit_solution(6295574927163842685)
XLA Ops:
  13.8 72.0 %all-gather.3.cloned.1.call-done = bf16[4608,512]{1,0:T(8,128)(2,1)} async-done(((bf16[144,512]{1,0:T(8,128)(2,1)}), bf16[4608,512]{1,0:T(8,128)(2,1)}) %all-gather.3.cloned.1.call-update) | async-done | bytes 4718608 | tf_op jit(solution)/shard_map/all_gather | solution.py:63
  101.4 545.1 %while.25 = (s32[]{:T(128)}, bf16[32,4096]{1,0:T(8,128)(2,1)}, bf16[10,32,4096]{2,1,0:T(8,128)(2,1)}, bf16[10,32,384]{2,1,0:T(8,128)(2,1)}, f32[4096]{0:T(1024)S...) while((s32[]{:T(128)}, bf16[32,4096]{1,0:T(8,128)(2,1)}, ...), condition=%wide.region_7.8_spmd.clone.clone.clone.clone, body=%wide.region_3.7_spmd.clone.clone.clone.clone.sunk | while | flops 137027552 | bytes 10679635 | solution.py:158
  113.3 5.0 collective-permute-start
  119.0 5.5 collective-permute-done
  137.0 7.9 collective-permute-start
  145.6 4.7 collective-permute-done
  162.9 7.9 collective-permute-start
  171.5 3.8 collective-permute-done
  187.8 7.9 collective-permute-start
  196.4 3.5 collective-permute-done
  212.4 7.9 collective-permute-start
  221.0 3.5 collective-permute-done
  237.0 7.9 collective-permute-start
  245.6 3.5 collective-permute-done
  261.6 7.9 collective-permute-start
  270.2 3.5 collective-permute-done
  286.2 7.9 collective-permute-start
  294.8 3.5 collective-permute-done
  310.7 7.9 collective-permute-start
  335.3 7.9 collective-permute-start
  343.9 3.5 collective-permute-done
  359.9 7.9 collective-permute-start
  368.5 3.5 collective-permute-done
  384.5 7.9 collective-permute-start
  409.1 7.9 collective-permute-start
  433.6 7.9 collective-permute-start
  442.2 3.5 collective-permute-done
  458.2 7.9 collective-permute-start
  466.8 3.5 collective-permute-done
  482.8 7.9 collective-permute-start
  491.4 3.5 collective-permute-done
  507.4 7.9 collective-permute-start
  516.0 3.5 collective-permute-done
  532.0 7.9 collective-permute-start
  540.6 3.5 collective-permute-done
  556.5 7.9 collective-permute-start
  565.2 3.5 collective-permute-done
  581.1 7.9 collective-permute-start
  589.7 4.6 collective-permute-done
  606.8 7.9 collective-permute-start
  615.4 5.8 collective-permute-done
  633.7 7.9 collective-permute-start
  642.3 3.6 collective-permute-done
  653.3 4.5 bitcast_convert_fusion
  661.5 4.6 pad_maximum_fusion
  666.1 6.5 copy.14
  675.8 34.2 %all-gather = f32[131072]{0:T(1024)S(1)} all-gather(f32[4096]{0:T(1024)S(1)} %select_add_fusion.1), channel_id=2, replica_groups=mesh['section'=16,'fsdp'=32] {'fsdp'}, dimensions={0}, use_global_device_ids=true | all-gather | bytes 540672 | tf_op jit(solution)/shard_map/all_gather | solution.py:179
  710.8 86.0 %reduce-scatter.4.cloned.1.call-done = bf16[128,512]{1,0:T(8,128)(2,1)} async-done(((bf16[4096,512]{1,0:T(8,128)(2,1)}), bf16[128,512]{1,0:T(8,128)(2,1)}) %reduce-scatter.4.cloned.1.call-update) | async-done | bytes 131088
  (465 shorter events, 338.7 us)
Async XLA Ops:
  7.2 4.1 copy-start.4
  7.2 78.6 %all-gather.3.cloned.1.call-start = ((), (), s32[]{:S(2)}) async-start(), calls=%async_computation.1 | async-start | bytes 4866048 | tf_op jit(solution)/shard_map/all_gather | solution.py:63
  9.0 787.9 %reduce-scatter.4.cloned.1.call-start = ((), (), s32[]{:S(2)}) async-start(), calls=%async_computation.2 | async-start | bytes 4325376
  88.4 2.4 copy-start
  89.3 2.5 copy-start.5
  93.2 0.8 copy-start.6
  94.1 7.3 copy-start.7
  94.1 7.3 copy-start.8
  94.1 7.3 copy-start.9
  94.1 7.3 copy-start.10
  113.3 11.2 %collective-permute-start = (bf16[32,4096]{1,0:T(8,128)(2,1)}, bf16[32,4096]{1,0:T(8,128)(2,1)S(1)}, u32[]{:S(2)}, u32[]{:S(2)}) collective-permute-start(bf16[32,4096]{1,0:T(8,128)(2,1)} %fusion.145), channel_id=1, source_target_pairs={{32,0},{64,32},{96,64},{128,96},{160,128},{192,160},{224,192},{256... | collective-permute-start | bytes 786440 | tf_op jit(solution)/shard_map/while/body/eval_jaxpr/ppermute | solution.py:10
  124.5 0.7 copy-start.1
  137.0 13.3 %collective-permute-start = (bf16[32,4096]{1,0:T(8,128)(2,1)}, bf16[32,4096]{1,0:T(8,128)(2,1)S(1)}, u32[]{:S(2)}, u32[]{:S(2)}) collective-permute-start(bf16[32,4096]{1,0:T(8,128)(2,1)} %fusion.145), channel_id=1, source_target_pairs={{32,0},{64,32},{96,64},{128,96},{160,128},{192,160},{224,192},{256... | collective-permute-start | bytes 786440 | tf_op jit(solution)/shard_map/while/body/eval_jaxpr/ppermute | solution.py:10
  150.4 0.7 copy-start.1
  162.9 12.4 %collective-permute-start = (bf16[32,4096]{1,0:T(8,128)(2,1)}, bf16[32,4096]{1,0:T(8,128)(2,1)S(1)}, u32[]{:S(2)}, u32[]{:S(2)}) collective-permute-start(bf16[32,4096]{1,0:T(8,128)(2,1)} %fusion.145), channel_id=1, source_target_pairs={{32,0},{64,32},{96,64},{128,96},{160,128},{192,160},{224,192},{256... | collective-permute-start | bytes 786440 | tf_op jit(solution)/shard_map/while/body/eval_jaxpr/ppermute | solution.py:10
  175.3 0.7 copy-start.1
  187.8 12.1 %collective-permute-start = (bf16[32,4096]{1,0:T(8,128)(2,1)}, bf16[32,4096]{1,0:T(8,128)(2,1)S(1)}, u32[]{:S(2)}, u32[]{:S(2)}) collective-permute-start(bf16[32,4096]{1,0:T(8,128)(2,1)} %fusion.145), channel_id=1, source_target_pairs={{32,0},{64,32},{96,64},{128,96},{160,128},{192,160},{224,192},{256... | collective-permute-start | bytes 786440 | tf_op jit(solution)/shard_map/while/body/eval_jaxpr/ppermute | solution.py:10
  199.9 0.7 copy-start.1
  212.4 12.1 %collective-permute-start = (bf16[32,4096]{1,0:T(8,128)(2,1)}, bf16[32,4096]{1,0:T(8,128)(2,1)S(1)}, u32[]{:S(2)}, u32[]{:S(2)}) collective-permute-start(bf16[32,4096]{1,0:T(8,128)(2,1)} %fusion.145), channel_id=1, source_target_pairs={{32,0},{64,32},{96,64},{128,96},{160,128},{192,160},{224,192},{256... | collective-permute-start | bytes 786440 | tf_op jit(solution)/shard_map/while/body/eval_jaxpr/ppermute | solution.py:10
  224.5 0.7 copy-start.1
  237.0 12.1 %collective-permute-start = (bf16[32,4096]{1,0:T(8,128)(2,1)}, bf16[32,4096]{1,0:T(8,128)(2,1)S(1)}, u32[]{:S(2)}, u32[]{:S(2)}) collective-permute-start(bf16[32,4096]{1,0:T(8,128)(2,1)} %fusion.145), channel_id=1, source_target_pairs={{32,0},{64,32},{96,64},{128,96},{160,128},{192,160},{224,192},{256... | collective-permute-start | bytes 786440 | tf_op jit(solution)/shard_map/while/body/eval_jaxpr/ppermute | solution.py:10
  249.1 0.7 copy-start.1
  261.6 12.1 %collective-permute-start = (bf16[32,4096]{1,0:T(8,128)(2,1)}, bf16[32,4096]{1,0:T(8,128)(2,1)S(1)}, u32[]{:S(2)}, u32[]{:S(2)}) collective-permute-start(bf16[32,4096]{1,0:T(8,128)(2,1)} %fusion.145), channel_id=1, source_target_pairs={{32,0},{64,32},{96,64},{128,96},{160,128},{192,160},{224,192},{256... | collective-permute-start | bytes 786440 | tf_op jit(solution)/shard_map/while/body/eval_jaxpr/ppermute | solution.py:10
  273.7 0.7 copy-start.1
  286.2 12.1 %collective-permute-start = (bf16[32,4096]{1,0:T(8,128)(2,1)}, bf16[32,4096]{1,0:T(8,128)(2,1)S(1)}, u32[]{:S(2)}, u32[]{:S(2)}) collective-permute-start(bf16[32,4096]{1,0:T(8,128)(2,1)} %fusion.145), channel_id=1, source_target_pairs={{32,0},{64,32},{96,64},{128,96},{160,128},{192,160},{224,192},{256... | collective-permute-start | bytes 786440 | tf_op jit(solution)/shard_map/while/body/eval_jaxpr/ppermute | solution.py:10
  298.3 0.7 copy-start.1
  310.7 12.1 %collective-permute-start = (bf16[32,4096]{1,0:T(8,128)(2,1)}, bf16[32,4096]{1,0:T(8,128)(2,1)S(1)}, u32[]{:S(2)}, u32[]{:S(2)}) collective-permute-start(bf16[32,4096]{1,0:T(8,128)(2,1)} %fusion.145), channel_id=1, source_target_pairs={{32,0},{64,32},{96,64},{128,96},{160,128},{192,160},{224,192},{256... | collective-permute-start | bytes 786440 | tf_op jit(solution)/shard_map/while/body/eval_jaxpr/ppermute | solution.py:10
  322.8 0.7 copy-start.1
  335.3 12.1 %collective-permute-start = (bf16[32,4096]{1,0:T(8,128)(2,1)}, bf16[32,4096]{1,0:T(8,128)(2,1)S(1)}, u32[]{:S(2)}, u32[]{:S(2)}) collective-permute-start(bf16[32,4096]{1,0:T(8,128)(2,1)} %fusion.145), channel_id=1, source_target_pairs={{32,0},{64,32},{96,64},{128,96},{160,128},{192,160},{224,192},{256... | collective-permute-start | bytes 786440 | tf_op jit(solution)/shard_map/while/body/eval_jaxpr/ppermute | solution.py:10
  359.9 12.1 %collective-permute-start = (bf16[32,4096]{1,0:T(8,128)(2,1)}, bf16[32,4096]{1,0:T(8,128)(2,1)S(1)}, u32[]{:S(2)}, u32[]{:S(2)}) collective-permute-start(bf16[32,4096]{1,0:T(8,128)(2,1)} %fusion.145), channel_id=1, source_target_pairs={{32,0},{64,32},{96,64},{128,96},{160,128},{192,160},{224,192},{256... | collective-permute-start | bytes 786440 | tf_op jit(solution)/shard_map/while/body/eval_jaxpr/ppermute | solution.py:10
  384.5 12.1 %collective-permute-start = (bf16[32,4096]{1,0:T(8,128)(2,1)}, bf16[32,4096]{1,0:T(8,128)(2,1)S(1)}, u32[]{:S(2)}, u32[]{:S(2)}) collective-permute-start(bf16[32,4096]{1,0:T(8,128)(2,1)} %fusion.145), channel_id=1, source_target_pairs={{32,0},{64,32},{96,64},{128,96},{160,128},{192,160},{224,192},{256... | collective-permute-start | bytes 786440 | tf_op jit(solution)/shard_map/while/body/eval_jaxpr/ppermute | solution.py:10
  396.5 0.7 copy-start.1
  409.1 12.1 %collective-permute-start = (bf16[32,4096]{1,0:T(8,128)(2,1)}, bf16[32,4096]{1,0:T(8,128)(2,1)S(1)}, u32[]{:S(2)}, u32[]{:S(2)}) collective-permute-start(bf16[32,4096]{1,0:T(8,128)(2,1)} %fusion.145), channel_id=1, source_target_pairs={{32,0},{64,32},{96,64},{128,96},{160,128},{192,160},{224,192},{256... | collective-permute-start | bytes 786440 | tf_op jit(solution)/shard_map/while/body/eval_jaxpr/ppermute | solution.py:10
  433.6 12.1 %collective-permute-start = (bf16[32,4096]{1,0:T(8,128)(2,1)}, bf16[32,4096]{1,0:T(8,128)(2,1)S(1)}, u32[]{:S(2)}, u32[]{:S(2)}) collective-permute-start(bf16[32,4096]{1,0:T(8,128)(2,1)} %fusion.145), channel_id=1, source_target_pairs={{32,0},{64,32},{96,64},{128,96},{160,128},{192,160},{224,192},{256... | collective-permute-start | bytes 786440 | tf_op jit(solution)/shard_map/while/body/eval_jaxpr/ppermute | solution.py:10
  445.7 0.7 copy-start.1
  458.2 12.1 %collective-permute-start = (bf16[32,4096]{1,0:T(8,128)(2,1)}, bf16[32,4096]{1,0:T(8,128)(2,1)S(1)}, u32[]{:S(2)}, u32[]{:S(2)}) collective-permute-start(bf16[32,4096]{1,0:T(8,128)(2,1)} %fusion.145), channel_id=1, source_target_pairs={{32,0},{64,32},{96,64},{128,96},{160,128},{192,160},{224,192},{256... | collective-permute-start | bytes 786440 | tf_op jit(solution)/shard_map/while/body/eval_jaxpr/ppermute | solution.py:10
  470.3 0.7 copy-start.1
  482.8 12.1 %collective-permute-start = (bf16[32,4096]{1,0:T(8,128)(2,1)}, bf16[32,4096]{1,0:T(8,128)(2,1)S(1)}, u32[]{:S(2)}, u32[]{:S(2)}) collective-permute-start(bf16[32,4096]{1,0:T(8,128)(2,1)} %fusion.145), channel_id=1, source_target_pairs={{32,0},{64,32},{96,64},{128,96},{160,128},{192,160},{224,192},{256... | collective-permute-start | bytes 786440 | tf_op jit(solution)/shard_map/while/body/eval_jaxpr/ppermute | solution.py:10
  507.4 12.1 %collective-permute-start = (bf16[32,4096]{1,0:T(8,128)(2,1)}, bf16[32,4096]{1,0:T(8,128)(2,1)S(1)}, u32[]{:S(2)}, u32[]{:S(2)}) collective-permute-start(bf16[32,4096]{1,0:T(8,128)(2,1)} %fusion.145), channel_id=1, source_target_pairs={{32,0},{64,32},{96,64},{128,96},{160,128},{192,160},{224,192},{256... | collective-permute-start | bytes 786440 | tf_op jit(solution)/shard_map/while/body/eval_jaxpr/ppermute | solution.py:10
  532.0 12.1 %collective-permute-start = (bf16[32,4096]{1,0:T(8,128)(2,1)}, bf16[32,4096]{1,0:T(8,128)(2,1)S(1)}, u32[]{:S(2)}, u32[]{:S(2)}) collective-permute-start(bf16[32,4096]{1,0:T(8,128)(2,1)} %fusion.145), channel_id=1, source_target_pairs={{32,0},{64,32},{96,64},{128,96},{160,128},{192,160},{224,192},{256... | collective-permute-start | bytes 786440 | tf_op jit(solution)/shard_map/while/body/eval_jaxpr/ppermute | solution.py:10
  556.5 12.1 %collective-permute-start = (bf16[32,4096]{1,0:T(8,128)(2,1)}, bf16[32,4096]{1,0:T(8,128)(2,1)S(1)}, u32[]{:S(2)}, u32[]{:S(2)}) collective-permute-start(bf16[32,4096]{1,0:T(8,128)(2,1)} %fusion.145), channel_id=1, source_target_pairs={{32,0},{64,32},{96,64},{128,96},{160,128},{192,160},{224,192},{256... | collective-permute-start | bytes 786440 | tf_op jit(solution)/shard_map/while/body/eval_jaxpr/ppermute | solution.py:10
  581.1 13.2 %collective-permute-start = (bf16[32,4096]{1,0:T(8,128)(2,1)}, bf16[32,4096]{1,0:T(8,128)(2,1)S(1)}, u32[]{:S(2)}, u32[]{:S(2)}) collective-permute-start(bf16[32,4096]{1,0:T(8,128)(2,1)} %fusion.145), channel_id=1, source_target_pairs={{32,0},{64,32},{96,64},{128,96},{160,128},{192,160},{224,192},{256... | collective-permute-start | bytes 786440 | tf_op jit(solution)/shard_map/while/body/eval_jaxpr/ppermute | solution.py:10
  606.8 14.4 %collective-permute-start = (bf16[32,4096]{1,0:T(8,128)(2,1)}, bf16[32,4096]{1,0:T(8,128)(2,1)S(1)}, u32[]{:S(2)}, u32[]{:S(2)}) collective-permute-start(bf16[32,4096]{1,0:T(8,128)(2,1)} %fusion.145), channel_id=1, source_target_pairs={{32,0},{64,32},{96,64},{128,96},{160,128},{192,160},{224,192},{256... | collective-permute-start | bytes 786440 | tf_op jit(solution)/shard_map/while/body/eval_jaxpr/ppermute | solution.py:10
  621.2 0.7 copy-start.1
  633.7 12.2 %collective-permute-start = (bf16[32,4096]{1,0:T(8,128)(2,1)}, bf16[32,4096]{1,0:T(8,128)(2,1)S(1)}, u32[]{:S(2)}, u32[]{:S(2)}) collective-permute-start(bf16[32,4096]{1,0:T(8,128)(2,1)} %fusion.145), channel_id=1, source_target_pairs={{32,0},{64,32},{96,64},{128,96},{160,128},{192,160},{224,192},{256... | collective-permute-start | bytes 786440 | tf_op jit(solution)/shard_map/while/body/eval_jaxpr/ppermute | solution.py:10
  653.3 4.5 copy-start.2
  653.3 4.5 copy-start.3
  653.3 5.6 copy-start.11
  (9 other events, 6.3 us)
Sparse Core Ops, SparseCore 0:
  10.7 75.0 all-gather.2
  672.7 124.0 reduce-scatter.3
where the time goes:
time: 816 us; the launch traced here: 806 us
  waiting for transfers between devices  242 us (30%)
  matrix products  175 us (21%)
  starting transfers between devices  171 us (21%)
  other arithmetic  117 us (14%)
  local copies, waits for them, and re-layouts  51.6 us (6%)
  blocking collectives  34.2 us (4%)
  between operations  14.3 us (2%)
    ppermute x22, starting transfers between devices, passed_along(): lax.ppermute(value, axis, [(source, source + steps) for source in range(l...  171 us
    unnamed x3, waiting for transfers between devices  86.1 us
    ppermute x22, waiting for transfers between devices, passed_along(): lax.ppermute(value, axis, [(source, source + steps) for source in range(l...  83.5 us
    dot_general x46, matrix products, contract_cols(): lax.dot_general(left, right, (((1,), (1,)), ((), ())), preferred_element_...  72.5 us
    all_gather x1, waiting for transfers between devices, on_device(): lax.all_gather(packed, 'fsdp', axis=0, tiled=True)  72 us
    dot_general x48, matrix products, contract_rows(): lax.dot_general(left, right, (((0,), (0,)), ((), ())), preferred_element_...  44.7 us
    convert_element_type x22, other arithmetic, tick(): grad_out = (grad_in.astype(jnp.float32) + grad_x).astype(jnp.bfloat16)  42.2 us
    dynamic_update_slice x23, other arithmetic, tick(): grad_store = lax.dynamic_update_index_in_dim(grad_store, grad_in, slot, 0)  40.8 us
  transfers between devices with their start and end apart: 24, of which 24 were waited for; matrix products, arithmetic and copies ran while one was open for 3% of the time, Pallas kernels for 0%

commit v1 on v0

--- a/solution.py
+++ b/solution.py
@@ -2,6 +2,11 @@
 import jax.numpy as jnp
 from jax import lax
 from jax.sharding import PartitionSpec as P
+
+
+def all_by_exchange(array, mesh_axis, d):
+    stack = jnp.stack([array] * lax.axis_size(mesh_axis))
+    return jnp.concatenate(lax.all_to_all(stack, mesh_axis, 0, 0), axis=d)
 
 
 def passed_along(value, axis, steps):
@@ -60,9 +65,7 @@
     gain_rows = jnp.zeros((16, weights.shape[2]), jnp.bfloat16)
     gain_rows = lax.dynamic_update_slice(gain_rows, gain[0][None, :], (0, 0))
     packed = jnp.concatenate([weights[0], gain_rows], axis=0)
-    gathered = lax.all_gather(packed, "fsdp", axis=0, tiled=True).reshape(
-        groups, rows_here + 16, weights.shape[2]
-    )
+    gathered = all_by_exchange(packed, "fsdp", 0).reshape(groups, rows_here + 16, weights.shape[2])
     w_full = gathered[:, :rows_here, :].reshape(groups * rows_here, weights.shape[2])
     gain_full = gathered[:, rows_here, :rows_here].reshape(groups * rows_here)
     wide_gain = gain_full.astype(jnp.float32)

time: 816 us -> 860 us (1.054)
  waiting for transfers between devices: 242 us -> 272 us
  starting transfers between devices: 171 us -> 183 us
    all_to_all x0 -> x1, waiting for transfers between devices: none -> 103 us  [all_by_exchange(): return jnp.concatenate(lax.all_to_all(stack, mesh_axis, 0, 0), axis=d)]
    all_gather x1 -> x0, waiting for transfers between devices: 72 us -> none  [on_device(): lax.all_gather(packed, 'fsdp', axis=0, tiled=True)]
    all_to_all x0 -> x1, starting transfers between devices: none -> 11.6 us  [all_by_exchange(): return jnp.concatenate(lax.all_to_all(stack, mesh_axis, 0, 0), axis=d)]
    unnamed x3 -> x2, waiting for transfers between devices: 86.1 us -> 85.4 us
where the time goes in v1:
time: 860 us; the launch traced here: 850 us
  waiting for transfers between devices  272 us (32%)
  starting transfers between devices  183 us (21%)
  matrix products  175 us (20%)
  other arithmetic  116 us (13%)
  local copies, waits for them, and re-layouts  53.4 us (6%)
  blocking collectives  35.3 us (4%)
  between operations  14.3 us (2%)
    ppermute x22, starting transfers between devices, passed_along(): lax.ppermute(value, axis, [(source, source + steps) for source in range(l...  171 us
    all_to_all x1, waiting for transfers between devices, all_by_exchange(): return jnp.concatenate(lax.all_to_all(stack, mesh_axis, 0, 0), axis=d)  103 us
    unnamed x2, waiting for transfers between devices  85.4 us
    ppermute x22, waiting for transfers between devices, passed_along(): lax.ppermute(value, axis, [(source, source + steps) for source in range(l...  83.5 us
    dot_general x46, matrix products, contract_cols(): lax.dot_general(left, right, (((1,), (1,)), ((), ())), preferred_element_...  72.5 us
    dot_general x48, matrix products, contract_rows(): lax.dot_general(left, right, (((0,), (0,)), ((), ())), preferred_element_...  44.7 us
    convert_element_type x22, other arithmetic, tick(): grad_out = (grad_in.astype(jnp.float32) + grad_x).astype(jnp.bfloat16)  42.2 us
    dynamic_update_slice x23, other arithmetic, tick(): grad_store = lax.dynamic_update_index_in_dim(grad_store, grad_in, slot, 0)  40.7 us
  transfers between devices with their start and end apart: 24, of which 24 were waited for; matrix products, arithmetic and copies ran while one was open for 3% of the time, Pallas kernels for 0%

profile of v1, /device:TPU:4, one launch (start us, length us, event | category | flops | bytes accessed | tf_op | source)
XLA Modules:
  0.0 849.6 jit_solution(18164398618521084972)
XLA Ops:
  10.8 11.6 %all-to-all-start = ((bf16[32,144,512]{2,1,0:T(8,128)(2,1)}), bf16[32,144,512]{2,1,0:T(8,128)(2,1)}, u32[]{:S(2)}, u32[]{:S(2)}) async-start(bf16[32,144,512]{2,1,0:T(8,128)(2,1)} %stack.2), calls=%async_computation | async-start | bytes 9437184 | tf_op jit(solution)/shard_map/all_to_all | solution.py:9
  25.7 103.3 %all-to-all-done = bf16[32,144,512]{2,1,0:T(8,128)(2,1)} async-done(((bf16[32,144,512]{2,1,0:T(8,128)(2,1)}), bf16[32,144,512]{2,1,0:T(8,128)(2,1)}, u32[]{:S(2)}, u32[]{:S(2)}) %all-to-all-start) | async-done | bytes 4718624 | tf_op jit(solution)/shard_map/all_to_all | solution.py:9
  144.5 545.7 %while.25 = (s32[]{:T(128)}, bf16[32,4096]{1,0:T(8,128)(2,1)}, bf16[10,32,4096]{2,1,0:T(8,128)(2,1)}, bf16[10,32,384]{2,1,0:T(8,128)(2,1)}, f32[4096]{0:T(1024)S...) while((s32[]{:T(128)}, bf16[32,4096]{1,0:T(8,128)(2,1)}, ...), condition=%wide.region_7.8_spmd.clone.clone.clone.clone, body=%wide.region_3.7_spmd.clone.clone.clone.clone.sunk | while | flops 137027552 | bytes 10679635 | solution.py:161
  156.3 5.6 collective-permute-start
  162.6 4.7 collective-permute-done
  179.9 7.9 collective-permute-start
  188.5 3.8 collective-permute-done
  204.8 7.9 collective-permute-start
  213.4 3.5 collective-permute-done
  229.4 7.9 collective-permute-start
  254.0 7.9 collective-permute-start
  278.5 7.9 collective-permute-start
  287.2 3.5 collective-permute-done
  303.1 7.9 collective-permute-start
  327.7 7.9 collective-permute-start
  336.3 3.5 collective-permute-done
  352.3 7.9 collective-permute-start
  360.8 3.5 collective-permute-done
  376.8 7.9 collective-permute-start
  385.4 3.5 collective-permute-done
  401.4 7.9 collective-permute-start
  410.0 3.5 collective-permute-done
  426.0 7.9 collective-permute-start
  434.6 3.5 collective-permute-done
  450.6 7.9 collective-permute-start
  459.2 3.5 collective-permute-done
  475.2 7.9 collective-permute-start
  499.8 7.9 collective-permute-start
  508.4 3.5 collective-permute-done
  524.3 7.9 collective-permute-start
  533.0 3.5 collective-permute-done
  548.9 7.9 collective-permute-start
  557.5 3.5 collective-permute-done
  573.5 7.9 collective-permute-start
  582.1 3.5 collective-permute-done
  598.1 7.9 collective-permute-start
  606.7 4.5 collective-permute-done
  623.8 7.9 collective-permute-start
  632.4 5.8 collective-permute-done
  650.6 7.9 collective-permute-start
  659.2 5.7 collective-permute-done
  677.4 7.9 collective-permute-start
  686.0 3.5 collective-permute-done
  696.9 4.5 bitcast_convert_fusion
  705.1 4.6 pad_maximum_fusion
  709.7 6.5 copy.14
  719.4 35.3 %all-gather = f32[131072]{0:T(1024)S(1)} all-gather(f32[4096]{0:T(1024)S(1)} %select_add_fusion.1), channel_id=2, replica_groups=mesh['section'=16,'fsdp'=32] {'fsdp'}, dimensions={0}, use_global_device_ids=true | all-gather | bytes 540672 | tf_op jit(solution)/shard_map/all_gather | solution.py:182
  755.5 85.4 %reduce-scatter.4.cloned.1.call-done = bf16[128,512]{1,0:T(8,128)(2,1)} async-done(((bf16[4096,512]{1,0:T(8,128)(2,1)}), bf16[128,512]{1,0:T(8,128)(2,1)}) %reduce-scatter.4.cloned.1.call-update) | async-done | bytes 131088
  (465 shorter events, 342.2 us)
Async XLA Ops:
  10.8 11.7 %copy-start.4 = (bf16[1,8,32,4096]{3,2,1,0:T(8,128)(2,1)S(1)}, bf16[1,8,32,4096]{3,2,1,0:T(8,128)(2,1)}, u32[]{:S(2)}) copy-start(bf16[1,8,32,4096]{3,2,1,0:T(8,128)(2,1)} %param.6) | copy-start | bytes 6291460
  10.8 118.2 %all-to-all-start = ((bf16[32,144,512]{2,1,0:T(8,128)(2,1)}), bf16[32,144,512]{2,1,0:T(8,128)(2,1)}, u32[]{:S(2)}, u32[]{:S(2)}) async-start(bf16[32,144,512]{2,1,0:T(8,128)(2,1)} %stack.2), calls=%async_computation | async-start | bytes 9437184 | tf_op jit(solution)/shard_map/all_to_all | solution.py:9
  22.4 818.5 %reduce-scatter.4.cloned.1.call-start = ((), (), s32[]{:S(2)}) async-start(), calls=%async_computation.2 | async-start | bytes 4325376
  131.7 3.1 copy-start
  131.7 3.1 copy-start.5
  136.1 0.8 copy-start.6
  137.0 7.4 copy-start.7
  137.1 7.4 copy-start.8
  137.1 7.4 copy-start.9
  137.1 7.4 copy-start.10
  156.3 11.1 %collective-permute-start = (bf16[32,4096]{1,0:T(8,128)(2,1)}, bf16[32,4096]{1,0:T(8,128)(2,1)S(1)}, u32[]{:S(2)}, u32[]{:S(2)}) collective-permute-start(bf16[32,4096]{1,0:T(8,128)(2,1)} %fusion.145), channel_id=1, source_target_pairs={{32,0},{64,32},{96,64},{128,96},{160,128},{192,160},{224,192},{256... | collective-permute-start | bytes 786440 | tf_op jit(solution)/shard_map/while/body/eval_jaxpr/ppermute | solution.py:15
  167.4 0.7 copy-start.1
  179.9 12.4 %collective-permute-start = (bf16[32,4096]{1,0:T(8,128)(2,1)}, bf16[32,4096]{1,0:T(8,128)(2,1)S(1)}, u32[]{:S(2)}, u32[]{:S(2)}) collective-permute-start(bf16[32,4096]{1,0:T(8,128)(2,1)} %fusion.145), channel_id=1, source_target_pairs={{32,0},{64,32},{96,64},{128,96},{160,128},{192,160},{224,192},{256... | collective-permute-start | bytes 786440 | tf_op jit(solution)/shard_map/while/body/eval_jaxpr/ppermute | solution.py:15
  192.3 0.7 copy-start.1
  204.8 12.1 %collective-permute-start = (bf16[32,4096]{1,0:T(8,128)(2,1)}, bf16[32,4096]{1,0:T(8,128)(2,1)S(1)}, u32[]{:S(2)}, u32[]{:S(2)}) collective-permute-start(bf16[32,4096]{1,0:T(8,128)(2,1)} %fusion.145), channel_id=1, source_target_pairs={{32,0},{64,32},{96,64},{128,96},{160,128},{192,160},{224,192},{256... | collective-permute-start | bytes 786440 | tf_op jit(solution)/shard_map/while/body/eval_jaxpr/ppermute | solution.py:15
  216.9 0.7 copy-start.1
  229.4 12.1 %collective-permute-start = (bf16[32,4096]{1,0:T(8,128)(2,1)}, bf16[32,4096]{1,0:T(8,128)(2,1)S(1)}, u32[]{:S(2)}, u32[]{:S(2)}) collective-permute-start(bf16[32,4096]{1,0:T(8,128)(2,1)} %fusion.145), channel_id=1, source_target_pairs={{32,0},{64,32},{96,64},{128,96},{160,128},{192,160},{224,192},{256... | collective-permute-start | bytes 786440 | tf_op jit(solution)/shard_map/while/body/eval_jaxpr/ppermute | solution.py:15
  241.5 0.7 copy-start.1
  254.0 12.1 %collective-permute-start = (bf16[32,4096]{1,0:T(8,128)(2,1)}, bf16[32,4096]{1,0:T(8,128)(2,1)S(1)}, u32[]{:S(2)}, u32[]{:S(2)}) collective-permute-start(bf16[32,4096]{1,0:T(8,128)(2,1)} %fusion.145), channel_id=1, source_target_pairs={{32,0},{64,32},{96,64},{128,96},{160,128},{192,160},{224,192},{256... | collective-permute-start | bytes 786440 | tf_op jit(solution)/shard_map/while/body/eval_jaxpr/ppermute | solution.py:15
  266.0 0.7 copy-start.1
  278.5 12.1 %collective-permute-start = (bf16[32,4096]{1,0:T(8,128)(2,1)}, bf16[32,4096]{1,0:T(8,128)(2,1)S(1)}, u32[]{:S(2)}, u32[]{:S(2)}) collective-permute-start(bf16[32,4096]{1,0:T(8,128)(2,1)} %fusion.145), channel_id=1, source_target_pairs={{32,0},{64,32},{96,64},{128,96},{160,128},{192,160},{224,192},{256... | collective-permute-start | bytes 786440 | tf_op jit(solution)/shard_map/while/body/eval_jaxpr/ppermute | solution.py:15
  290.6 0.7 copy-start.1
  303.1 12.1 %collective-permute-start = (bf16[32,4096]{1,0:T(8,128)(2,1)}, bf16[32,4096]{1,0:T(8,128)(2,1)S(1)}, u32[]{:S(2)}, u32[]{:S(2)}) collective-permute-start(bf16[32,4096]{1,0:T(8,128)(2,1)} %fusion.145), channel_id=1, source_target_pairs={{32,0},{64,32},{96,64},{128,96},{160,128},{192,160},{224,192},{256... | collective-permute-start | bytes 786440 | tf_op jit(solution)/shard_map/while/body/eval_jaxpr/ppermute | solution.py:15
  315.2 0.7 copy-start.1
  327.7 12.1 %collective-permute-start = (bf16[32,4096]{1,0:T(8,128)(2,1)}, bf16[32,4096]{1,0:T(8,128)(2,1)S(1)}, u32[]{:S(2)}, u32[]{:S(2)}) collective-permute-start(bf16[32,4096]{1,0:T(8,128)(2,1)} %fusion.145), channel_id=1, source_target_pairs={{32,0},{64,32},{96,64},{128,96},{160,128},{192,160},{224,192},{256... | collective-permute-start | bytes 786440 | tf_op jit(solution)/shard_map/while/body/eval_jaxpr/ppermute | solution.py:15
  339.8 0.7 copy-start.1
  352.3 12.1 %collective-permute-start = (bf16[32,4096]{1,0:T(8,128)(2,1)}, bf16[32,4096]{1,0:T(8,128)(2,1)S(1)}, u32[]{:S(2)}, u32[]{:S(2)}) collective-permute-start(bf16[32,4096]{1,0:T(8,128)(2,1)} %fusion.145), channel_id=1, source_target_pairs={{32,0},{64,32},{96,64},{128,96},{160,128},{192,160},{224,192},{256... | collective-permute-start | bytes 786440 | tf_op jit(solution)/shard_map/while/body/eval_jaxpr/ppermute | solution.py:15
  364.3 0.7 copy-start.1
  376.8 12.1 %collective-permute-start = (bf16[32,4096]{1,0:T(8,128)(2,1)}, bf16[32,4096]{1,0:T(8,128)(2,1)S(1)}, u32[]{:S(2)}, u32[]{:S(2)}) collective-permute-start(bf16[32,4096]{1,0:T(8,128)(2,1)} %fusion.145), channel_id=1, source_target_pairs={{32,0},{64,32},{96,64},{128,96},{160,128},{192,160},{224,192},{256... | collective-permute-start | bytes 786440 | tf_op jit(solution)/shard_map/while/body/eval_jaxpr/ppermute | solution.py:15
  388.9 0.7 copy-start.1
  401.4 12.1 %collective-permute-start = (bf16[32,4096]{1,0:T(8,128)(2,1)}, bf16[32,4096]{1,0:T(8,128)(2,1)S(1)}, u32[]{:S(2)}, u32[]{:S(2)}) collective-permute-start(bf16[32,4096]{1,0:T(8,128)(2,1)} %fusion.145), channel_id=1, source_target_pairs={{32,0},{64,32},{96,64},{128,96},{160,128},{192,160},{224,192},{256... | collective-permute-start | bytes 786440 | tf_op jit(solution)/shard_map/while/body/eval_jaxpr/ppermute | solution.py:15
  426.0 12.1 %collective-permute-start = (bf16[32,4096]{1,0:T(8,128)(2,1)}, bf16[32,4096]{1,0:T(8,128)(2,1)S(1)}, u32[]{:S(2)}, u32[]{:S(2)}) collective-permute-start(bf16[32,4096]{1,0:T(8,128)(2,1)} %fusion.145), channel_id=1, source_target_pairs={{32,0},{64,32},{96,64},{128,96},{160,128},{192,160},{224,192},{256... | collective-permute-start | bytes 786440 | tf_op jit(solution)/shard_map/while/body/eval_jaxpr/ppermute | solution.py:15
  450.6 12.1 %collective-permute-start = (bf16[32,4096]{1,0:T(8,128)(2,1)}, bf16[32,4096]{1,0:T(8,128)(2,1)S(1)}, u32[]{:S(2)}, u32[]{:S(2)}) collective-permute-start(bf16[32,4096]{1,0:T(8,128)(2,1)} %fusion.145), channel_id=1, source_target_pairs={{32,0},{64,32},{96,64},{128,96},{160,128},{192,160},{224,192},{256... | collective-permute-start | bytes 786440 | tf_op jit(solution)/shard_map/while/body/eval_jaxpr/ppermute | solution.py:15
  475.2 12.1 %collective-permute-start = (bf16[32,4096]{1,0:T(8,128)(2,1)}, bf16[32,4096]{1,0:T(8,128)(2,1)S(1)}, u32[]{:S(2)}, u32[]{:S(2)}) collective-permute-start(bf16[32,4096]{1,0:T(8,128)(2,1)} %fusion.145), channel_id=1, source_target_pairs={{32,0},{64,32},{96,64},{128,96},{160,128},{192,160},{224,192},{256... | collective-permute-start | bytes 786440 | tf_op jit(solution)/shard_map/while/body/eval_jaxpr/ppermute | solution.py:15
  487.3 0.7 copy-start.1
  499.8 12.1 %collective-permute-start = (bf16[32,4096]{1,0:T(8,128)(2,1)}, bf16[32,4096]{1,0:T(8,128)(2,1)S(1)}, u32[]{:S(2)}, u32[]{:S(2)}) collective-permute-start(bf16[32,4096]{1,0:T(8,128)(2,1)} %fusion.145), channel_id=1, source_target_pairs={{32,0},{64,32},{96,64},{128,96},{160,128},{192,160},{224,192},{256... | collective-permute-start | bytes 786440 | tf_op jit(solution)/shard_map/while/body/eval_jaxpr/ppermute | solution.py:15
  524.3 12.1 %collective-permute-start = (bf16[32,4096]{1,0:T(8,128)(2,1)}, bf16[32,4096]{1,0:T(8,128)(2,1)S(1)}, u32[]{:S(2)}, u32[]{:S(2)}) collective-permute-start(bf16[32,4096]{1,0:T(8,128)(2,1)} %fusion.145), channel_id=1, source_target_pairs={{32,0},{64,32},{96,64},{128,96},{160,128},{192,160},{224,192},{256... | collective-permute-start | bytes 786440 | tf_op jit(solution)/shard_map/while/body/eval_jaxpr/ppermute | solution.py:15
  548.9 12.1 %collective-permute-start = (bf16[32,4096]{1,0:T(8,128)(2,1)}, bf16[32,4096]{1,0:T(8,128)(2,1)S(1)}, u32[]{:S(2)}, u32[]{:S(2)}) collective-permute-start(bf16[32,4096]{1,0:T(8,128)(2,1)} %fusion.145), channel_id=1, source_target_pairs={{32,0},{64,32},{96,64},{128,96},{160,128},{192,160},{224,192},{256... | collective-permute-start | bytes 786440 | tf_op jit(solution)/shard_map/while/body/eval_jaxpr/ppermute | solution.py:15
  561.0 0.7 copy-start.1
  573.5 12.1 %collective-permute-start = (bf16[32,4096]{1,0:T(8,128)(2,1)}, bf16[32,4096]{1,0:T(8,128)(2,1)S(1)}, u32[]{:S(2)}, u32[]{:S(2)}) collective-permute-start(bf16[32,4096]{1,0:T(8,128)(2,1)} %fusion.145), channel_id=1, source_target_pairs={{32,0},{64,32},{96,64},{128,96},{160,128},{192,160},{224,192},{256... | collective-permute-start | bytes 786440 | tf_op jit(solution)/shard_map/while/body/eval_jaxpr/ppermute | solution.py:15
  598.1 13.2 %collective-permute-start = (bf16[32,4096]{1,0:T(8,128)(2,1)}, bf16[32,4096]{1,0:T(8,128)(2,1)S(1)}, u32[]{:S(2)}, u32[]{:S(2)}) collective-permute-start(bf16[32,4096]{1,0:T(8,128)(2,1)} %fusion.145), channel_id=1, source_target_pairs={{32,0},{64,32},{96,64},{128,96},{160,128},{192,160},{224,192},{256... | collective-permute-start | bytes 786440 | tf_op jit(solution)/shard_map/while/body/eval_jaxpr/ppermute | solution.py:15
  623.8 14.4 %collective-permute-start = (bf16[32,4096]{1,0:T(8,128)(2,1)}, bf16[32,4096]{1,0:T(8,128)(2,1)S(1)}, u32[]{:S(2)}, u32[]{:S(2)}) collective-permute-start(bf16[32,4096]{1,0:T(8,128)(2,1)} %fusion.145), channel_id=1, source_target_pairs={{32,0},{64,32},{96,64},{128,96},{160,128},{192,160},{224,192},{256... | collective-permute-start | bytes 786440 | tf_op jit(solution)/shard_map/while/body/eval_jaxpr/ppermute | solution.py:15
  638.1 0.7 copy-start.1
  650.6 14.3 %collective-permute-start = (bf16[32,4096]{1,0:T(8,128)(2,1)}, bf16[32,4096]{1,0:T(8,128)(2,1)S(1)}, u32[]{:S(2)}, u32[]{:S(2)}) collective-permute-start(bf16[32,4096]{1,0:T(8,128)(2,1)} %fusion.145), channel_id=1, source_target_pairs={{32,0},{64,32},{96,64},{128,96},{160,128},{192,160},{224,192},{256... | collective-permute-start | bytes 786440 | tf_op jit(solution)/shard_map/while/body/eval_jaxpr/ppermute | solution.py:15
  677.4 12.1 %collective-permute-start = (bf16[32,4096]{1,0:T(8,128)(2,1)}, bf16[32,4096]{1,0:T(8,128)(2,1)S(1)}, u32[]{:S(2)}, u32[]{:S(2)}) collective-permute-start(bf16[32,4096]{1,0:T(8,128)(2,1)} %fusion.145), channel_id=1, source_target_pairs={{32,0},{64,32},{96,64},{128,96},{160,128},{192,160},{224,192},{256... | collective-permute-start | bytes 786440 | tf_op jit(solution)/shard_map/while/body/eval_jaxpr/ppermute | solution.py:15
  696.9 4.5 copy-start.2
  696.9 4.5 copy-start.3
  696.9 5.6 copy-start.11
  (9 other events, 6.3 us)
Sparse Core Ops, SparseCore 0:
  716.3 124.5 reduce-scatter.3
